TPU v7x, 128 devices: a whole 4x4x4 slice. The times are simulated.
128 devices in a mesh: rng: 8 (over z, y_hi), az: 16 (over y_lo, x, core).
Axes of the slice: x: 4, y: 4 (y_hi: 2, y_lo: 2; y = y_hi * 2 + y_lo), z: 4, core: 2. Of those that a mesh axis runs over, the one named last changes fastest.
Arguments:
- raw_swath: bfloat16 [8192, 2, 16384], P('rng', None, 'az'), may hold values from -6 to 6
- azimuth_filter: bfloat16 [8192, 2, 16384], P(('rng', 'az')), may hold values from -4 to 4
- anchors: int32 [8, 63, 2], replicated, may hold values from 0 to 15872, as said below
- owners: int32 [8, 63], replicated, may hold values from 0 to 15, as said below
- look_bands: int32 [8, 63, 3], replicated, may hold values from 0 to 384
Outputs:
- cross_spectra: float32 [8, 64, 2, 512, 128], P('rng', 'az')
Inputs may be any that keep to these rules, and one draw needn't show every extreme that they name: anchors[r, i] is the first line and the first column (in units of 64 cells) of imagette i in strip r; the column is below 16, and below 9 in the last strip; some imagette of each strip starts at line 16384 - 512. `owners`: in each strip every owner appears at most 4 times, and all but one owner exactly 4 times.
All inputs are finite; a program needn't handle non-finite values.
Results may differ from a plain program's by a relative error of at most 0.004.
Values may be sent and summed in bfloat16 or wider, within the bound.
No kernel may reach another device: no remote copies, remote signals or barrier semaphores. Data moves between devices by JAX's collectives and lax.ppermute only.
A program may use at most 128 MiB of HBM per device.

v0:
```python
import math

import jax
import jax.numpy as jnp
import numpy as np
from jax import lax
from jax.experimental import pallas as pl
from jax.experimental.pallas import tpu as pltpu
from jax.sharding import PartitionSpec as P


AZ_OUTER = 128
AZ_INNER = 128
LINES = 16384
IMG_C = 512
IMG_L = 512
LOOK = 128
COL = 64
IMG_DEV = 4
SPAN = IMG_C // COL
BLOCK = 16
TURN_ROWS = 32
HALF = COL // 2
DEEP = 2
NEAR = 2
epsilon = 1e-06
bf16 = jnp.bfloat16
f32 = jnp.float32


def dft_np(length, sign):
    steps = np.arange(length)
    phase = (steps[:, None] * steps[None, :]) % length
    angle = 2.0 * math.pi * phase / length
    scale = 1.0 / math.sqrt(length)
    return np.cos(angle) * scale, sign * np.sin(angle) * scale


def low(table):
    return np.asarray(table, np.float32).astype(jnp.bfloat16)


def left_form(length, sign):
    re, im = dft_np(length, sign)
    return low(np.block([[re, -im], [im, re]]))


def right_form(length, sign):
    re, im = dft_np(length, sign)
    return low(np.block([[re, im], [-im, re]]))


def twiddles():
    steps = np.arange(AZ_OUTER)
    angle = 2.0 * math.pi * ((steps[:, None] * steps[None, :]) % LINES) / LINES
    return np.stack([np.cos(angle), -np.sin(angle)]).astype(np.float32)


def in_vmem(*values):
    return [pltpu.with_memory_space_constraint(value, pltpu.VMEM) for value in values]


def dot(left, right):
    return jnp.dot(left, right, preferred_element_type=f32)


def focus_kernel(beyond_ref, own_ref, *refs, steps, turns):
    arr_ref, filt_ref, l1_ref, t2_ref, t3_ref, l4_ref, tw_ref, w_ref, near_ref, far_ref, kept_ref = refs[:11]
    y_ref, lines_ref, list_ref, *spec_refs = refs[11:]
    step = pl.program_id(0)

    @pl.when(step < steps)
    def _():
        tw_re = tw_ref[0]
        tw_im = tw_ref[1]
        pairs = range(BLOCK // 2)

        def stacked(cell):
            return jnp.concatenate(
                [arr_ref[:, cell, part].reshape(AZ_OUTER, AZ_INNER) for part in (0, 1)], axis=0
            )

        sections = []
        for pair in pairs:
            out = dot(l1_ref[...], jnp.concatenate([stacked(2 * pair), stacked(2 * pair + 1)], axis=1))
            rows = []
            for half in (0, 1):
                re = out[:128, half * 128 : half * 128 + 128]
                im = out[128:, half * 128 : half * 128 + 128]
                rows.append(
                    jnp.concatenate([re * tw_re - im * tw_im, re * tw_im + im * tw_re], axis=1).astype(bf16)
                )
            sections.append(jnp.concatenate(rows, axis=0))
        spectra = []
        for pair in pairs:
            out = dot(sections[pair], t2_ref[...])
            rows = []
            for half in (0, 1):
                re = out[half * 128 : half * 128 + 128, :128]
                im = out[half * 128 : half * 128 + 128, 128:]
                g_re = filt_ref[2 * pair + half, 0].astype(f32)
                g_im = filt_ref[2 * pair + half, 1].astype(f32)
                rows.append(
                    jnp.concatenate([re * g_re - im * g_im, re * g_im + im * g_re], axis=1).astype(bf16)
                )
            spectra.append(jnp.concatenate(rows, axis=0))
        rests = []
        for pair in pairs:
            out = dot(spectra[pair], t3_ref[...])
            columns = []
            for half in (0, 1):
                re = out[half * 128 : half * 128 + 128, :128]
                im = out[half * 128 : half * 128 + 128, 128:]
                columns.append(
                    jnp.concatenate([re * tw_re + im * tw_im, im * tw_re - re * tw_im], axis=0).astype(bf16)
                )
            rests.append(jnp.concatenate(columns, axis=1))
        for pair in pairs:
            out = dot(l4_ref[...], rests[pair])
            for half in (0, 1):
                cell = step * BLOCK + 2 * pair + half
                y_ref[pl.ds(cell * 128, 128), :] = out[:128, half * 128 : half * 128 + 128]
                y_ref[pl.ds((HALF + cell) * 128, 128), :] = out[128:, half * 128 : half * 128 + 128]

    @pl.when(step >= steps)
    def _():
        first = (step - steps) * TURN_ROWS
        for row in range(TURN_ROWS):
            block = y_ref[pl.ds(first + row, 2 * HALF, stride=128), :]
            block = jnp.concatenate([block[:HALF], block[:HALF], block[HALF:], block[HALF:]], axis=0)
            value = block.T.astype(bf16).astype(f32)
            lines_ref[pl.ds(pl.multiple_of((first + row) * 128, 128), 128), :] = value

    @pl.when(step == steps + turns - 1)
    def _():
        for info_ref, outs in ((beyond_ref, (near_ref, far_ref)), (own_ref, (kept_ref,))):
            trips = listed_trips(info_ref, list_ref)
            look_trips(trips, info_ref, list_ref, lines_ref, spec_refs, w_ref, l4_ref, outs)


def focus(beyond, own, arrived, response, half):
    steps = HALF // BLOCK
    turns = AZ_OUTER // TURN_ROWS
    whole = lambda shape: pl.BlockSpec(shape, lambda i, *s: (0,) * len(shape))
    shapes = [(16, looks, LOOK, 128) for looks in (NEAR, 3 - NEAR, 3)]
    return pl.pallas_call(
        lambda *refs: focus_kernel(*refs, steps=steps, turns=turns),
        out_shape=[jax.ShapeDtypeStruct(shape, bf16) for shape in shapes],
        grid_spec=pltpu.PrefetchScalarGridSpec(
            num_scalar_prefetch=2,
            grid=(steps + turns,),
            in_specs=[
                pl.BlockSpec((16, BLOCK, 2, 8, 128), lambda i, *s: (0, jnp.minimum(i, steps - 1), 0, 0, 0)),
                pl.BlockSpec(
                    (BLOCK, 2, 128, 128), lambda i, *s: (half * steps + jnp.minimum(i, steps - 1), 0, 0, 0)
                ),
                whole((256, 256)),
                whole((256, 256)),
                whole((256, 256)),
                whole((256, 256)),
                whole((2, 128, 128)),
                whole((IMG_L, 2 * IMG_L)),
            ],
            out_specs=[whole(shape) for shape in shapes],
            scratch_shapes=[
                pltpu.VMEM((2 * HALF * 128, 128), f32),
                pltpu.VMEM((LINES, 128), f32),
                pltpu.SMEM((IMG_DEV * (16 + 2 * DEEP),), jnp.int32),
            ]
            + [pltpu.VMEM((2 * IMG_L, 128), f32)] * DEEP,
        ),
    )(
        beyond,
        own,
        arrived,
        response,
        jnp.asarray(left_form(128, -1.0)),
        jnp.asarray(right_form(128, -1.0)),
        jnp.asarray(right_form(128, 1.0)),
        jnp.asarray(left_form(128, 1.0)),
        jnp.asarray(twiddles()),
        window_table(),
    )


def listed_trips(info_ref, list_ref):
    owners = 16
    room = owners + 2 * DEEP
    most = 0
    for slot in range(IMG_DEV):
        for place in range(room):
            list_ref[slot * room + place] = 0
        found = 0
        for owner in range(owners):
            list_ref[slot * room + found] = owner
            found = found + info_ref[(owner * IMG_DEV + slot) * 8 + 1]
        most = jnp.maximum(most, found)
    return (most + DEEP - 1) // DEEP


def look_trips(trips, info_ref, list_ref, lines_ref, spec_refs, w_ref, u_ref, outs):
    room = 16 + 2 * DEEP
    lane = lax.broadcasted_iota(jnp.int32, (1, 128), 1)
    low_lanes = lane < 64
    sign = jnp.where(low_lanes, 1.0, -1.0).astype(f32)
    even = lane % 64 < 32
    split = len(outs) > 1

    def chosen(tiles):
        return jnp.where(low_lanes, jnp.where(even, tiles[0], tiles[1]), jnp.where(even, tiles[2], tiles[3]))

    def trip(at, carry):
        picks = [
            [list_ref[slot * room + DEEP * at + nth] for slot in range(IMG_DEV)] for nth in range(DEEP)
        ]
        places = [[(owner * IMG_DEV + slot) * 8 for slot, owner in enumerate(row)] for row in picks]
        for nth in range(DEEP):
            images = [lines_ref[pl.ds(info_ref[place], IMG_L), :] for place in places[nth]]
            near = jnp.where(even, images[0], images[1])
            far = jnp.where(even, images[2], images[3])
            side = pltpu.roll(jnp.where(low_lanes, far, near), 64, 1) * sign
            main = jnp.where(low_lanes, near, far).astype(bf16)
            right = jnp.concatenate(
                [
                    jnp.concatenate([main, side.astype(bf16)], axis=1),
                    jnp.concatenate([(-side).astype(bf16), main], axis=1),
                ],
                axis=0,
            )
            spectra = dot(w_ref[...], right)
            spec_refs[nth][:IMG_L, :] = spectra[:, :128]
            spec_refs[nth][IMG_L:, :] = spectra[:, 128:]
        for nth in range(DEEP):
            columns = []
            for look in range(3):
                parts = []
                for part in (0, 1):
                    tiles = [
                        spec_refs[nth][pl.ds(part * IMG_L + info_ref[place + 2 + look], LOOK), :]
                        for place in places[nth]
                    ]
                    parts.append(chosen(tiles).astype(bf16))
                columns.append(jnp.concatenate(parts, axis=0))
            value = dot(u_ref[...], jnp.concatenate(columns, axis=1))
            for look in range(3):
                re = value[:LOOK, look * 128 : look * 128 + 128]
                im = value[LOOK:, look * 128 : look * 128 + 128]
                power = (re * re + im * im).astype(bf16)
                for slot, owner in enumerate(picks[nth]):
                    lanes = slice(slot * HALF, slot * HALF + HALF)
                    if split and look >= NEAR:
                        outs[1][owner, look - NEAR, :, lanes] = power[:, lanes]
                    else:
                        outs[0][owner, look, :, lanes] = power[:, lanes]
        return carry

    lax.fori_loop(0, trips, trip, 0)


def window_table():
    return jnp.asarray(low(np.concatenate(dft_np(IMG_L, -1.0), axis=1)))


def merge_kernel(flag_ref, own_ref, near_ref, far_ref, out_ref):
    lane = lax.broadcasted_iota(jnp.int32, (1, 1, 128), 2)

    def one(owner, carry):
        for part, other_ref in enumerate((near_ref, far_ref)):
            looks = slice(part * NEAR, 3 if part else NEAR)
            taken = 0
            for slot in range(IMG_DEV):
                flag = flag_ref[(owner * IMG_DEV + slot) * 2 + part]
                taken = jnp.where(lane // HALF == slot, flag, taken)
            own = own_ref[owner, looks].astype(f32)
            out_ref[owner, looks] = jnp.where(taken > 0, other_ref[owner].astype(f32), own).astype(bf16)
        return carry

    lax.fori_loop(0, 16, one, 0)


def merged(flags, own, near, far):
    inside = pl.BlockSpec(memory_space=pltpu.VMEM)
    return pl.pallas_call(
        merge_kernel,
        out_shape=jax.ShapeDtypeStruct(own.shape, bf16),
        in_specs=[pl.BlockSpec(memory_space=pltpu.SMEM), inside, inside, inside],
        out_specs=inside,
        compiler_params=pltpu.CompilerParams(vmem_limit_bytes=16 << 20),
    )(flags, own, near, far)


def cross_kernel(info_ref, first_ref, second_ref, w_ref, l_ref, out_ref):
    step = pl.program_id(0)
    lane = lax.broadcasted_iota(jnp.int32, (1, 128), 1)
    for nth in (0, 1):
        slot = 2 * step + nth
        start = info_ref[slot * 2]
        filled = info_ref[slot * 2 + 1] > 0
        rows = []
        for look in range(3):

            def piece(at, half):
                column = start + at
                ref = second_ref if half else first_ref
                source = jnp.where(column < 16, column, column - (8 if look < NEAR else 16))
                return ref[source, look].astype(f32)

            pieces = []
            for part in range(SPAN // 2):
                joined = None
                for spot in range(4):
                    value = piece(2 * part + spot // 2, spot % 2)
                    value = pltpu.roll(value, (HALF * (spot - slot)) % 128, 1)
                    joined = value if spot == 0 else jnp.where(lane < HALF * spot, joined, value)
                pieces.append(joined)
            power = jnp.concatenate(pieces, axis=1)
            mean = jnp.sum(power) * (1.0 / (IMG_C * LOOK))
            rows.append((power * (1.0 / (mean + epsilon)) - 1.0).astype(bf16))
        across = dot(jnp.concatenate(rows, axis=0), w_ref[...]).astype(bf16)
        waves = []
        for look in range(3):
            part = across[look * 128 : look * 128 + 128]
            both = jnp.concatenate([part[:, :IMG_C], part[:, IMG_C:]], axis=0)
            value = dot(l_ref[...], both)
            waves.append((value[:128], value[128:]))
        one_re, one_im = waves[0]
        two_re, two_im = waves[1]
        three_re, three_im = waves[2]
        sum_re = two_re + three_re
        sum_im = two_im + three_im
        total_re = one_re * sum_re + one_im * sum_im + (two_re * three_re + two_im * three_im)
        total_im = one_im * sum_re - one_re * sum_im + (two_im * three_re - two_re * three_im)
        out_ref[nth, 0] = jnp.where(filled, total_re, 0.0).T
        out_ref[nth, 1] = jnp.where(filled, total_im, 0.0).T


def cross(info, first, second):
    whole = lambda shape: pl.BlockSpec(shape, lambda i, s: (0,) * len(shape))
    return pl.pallas_call(
        cross_kernel,
        out_shape=jax.ShapeDtypeStruct((IMG_DEV, 2, IMG_C, LOOK), f32),
        grid_spec=pltpu.PrefetchScalarGridSpec(
            num_scalar_prefetch=1,
            grid=(2,),
            in_specs=[
                pl.BlockSpec(memory_space=pltpu.VMEM),
                pl.BlockSpec(memory_space=pltpu.VMEM),
                whole((IMG_C, 2 * IMG_C)),
                whole((256, 256)),
            ],
            out_specs=pl.BlockSpec((2, 2, IMG_C, LOOK), lambda i, s: (i, 0, 0, 0)),
        ),
        compiler_params=pltpu.CompilerParams(vmem_limit_bytes=40 << 20),
        name="cross",
    )(
        info,
        first,
        second,
        window_table(),
        jnp.asarray(left_form(128, -1.0)),
    )


def strip_facts(anchors, owners, look_bands, strip, count):
    row = lax.dynamic_index_in_dim(owners, strip, 0, keepdims=False)
    facts = jnp.concatenate(
        [
            lax.dynamic_index_in_dim(anchors, strip, 0, keepdims=False),
            lax.dynamic_index_in_dim(look_bands, strip, 0, keepdims=False),
        ],
        axis=1,
    )
    items = jnp.arange(row.shape[0], dtype=jnp.int32)
    earlier = (row[:, None] == row[None, :]) & (items[None, :] < items[:, None])
    rank = jnp.sum(earlier.astype(jnp.int32), axis=1)
    place = row * IMG_DEV + rank
    slots = jnp.arange(count * IMG_DEV, dtype=jnp.int32)
    hot = (place[None, :] == slots[:, None]).astype(jnp.int32)
    filled = jnp.sum(hot, axis=1)
    chosen = jnp.sum(hot[:, :, None] * facts[None], axis=1)
    line = jnp.clip(chosen[:, 0], 0, LINES - IMG_L)
    bands = jnp.clip(chosen[:, 2:], 0, IMG_L - LOOK)
    return line, chosen[:, 1], bands, filled


def reaches(start, filled, column):
    return ((start <= column) & (column < start + SPAN) & (filled > 0)).astype(jnp.int32)


def listed(line, bands, keep):
    pad = jnp.zeros((keep.shape[0], 3), jnp.int32)
    return jnp.concatenate([line[:, None], keep[:, None], bands, pad], axis=1).reshape(-1)


def staged(raw_swath, azimuth_filter, anchors, owners, look_bands):
    count = lax.axis_size("az")
    strips = lax.axis_size("rng")
    strip = lax.axis_index("rng")
    column = lax.axis_index("az")
    line, start, bands, filled = strip_facts(anchors, owners, look_bands, strip, count)
    own = listed(line, bands, reaches(start, filled, column))
    flags = jnp.stack(
        [
            reaches(start, filled, column + SPAN) * (column >= SPAN).astype(jnp.int32),
            reaches(start, filled, column + count),
        ],
        axis=1,
    ).reshape(-1)
    mine = jnp.stack([start, filled], axis=1)
    mine = lax.dynamic_slice_in_dim(mine, column * IMG_DEV, IMG_DEV, 0).reshape(-1)
    line, start, bands, filled = strip_facts(
        anchors, owners, look_bands, jnp.maximum(strip - 1, 0), count
    )
    keep = reaches(start, filled, column + count) * (strip > 0).astype(jnp.int32)
    beyond = listed(line, bands, keep)

    response = azimuth_filter.reshape(COL, 2, AZ_OUTER, AZ_INNER)
    reach = [
        [((r + 1) * count + c, r * count + c + shift) for r in range(strips - 1) for c in range(SPAN - 1)]
        for shift in (SPAN, 0)
    ]
    arrived = []
    chosen = None
    for half in (0, 1):
        if half:
            raw_swath, _ = lax.optimization_barrier((raw_swath, chosen))
        pieces = raw_swath.reshape(count, COL, 2, raw_swath.shape[2])
        chosen = pieces[:, half * HALF : half * HALF + HALF].reshape(count, HALF, 2, 8, 128)
        arrived.append(lax.all_to_all(chosen, "az", split_axis=0, concat_axis=0, tiled=True))
    kept = []
    passed = []
    for half in (0, 1):
        *parts, mine_part = focus(beyond, own, arrived[half], response, half)
        kept.append(mine_part)
        for way in (0, 1):
            passed.append(lax.ppermute(parts[way], ("rng", "az"), reach[way]))
    powers = []
    for half in (0, 1):
        joined = merged(flags, kept[half], *passed[2 * half : 2 * half + 2])
        powers.append(lax.all_to_all(joined, "az", split_axis=0, concat_axis=0, tiled=True))
    return cross(mine, *in_vmem(*powers))[None]


def solution(mesh):
    in_specs = (P("rng", None, "az"), P(("rng", "az"), None, None), P(), P(), P())
    out_specs = P("rng", "az", None, None, None)
    return jax.shard_map(staged, mesh=mesh, in_specs=in_specs, out_specs=out_specs, check_vma=False)
```

profile of v0, /device:TPU:50, one launch (start us, length us, event | category | flops | bytes accessed | tf_op | source)
XLA Modules:
  0.0 200.4 jit_solution(6006637861956945423)
XLA Ops:
  0.0 3.1 %slice.32 = bf16[16,32,2,1024]{3,2,1,0:T(2,128)(2,1)S(1)} slice(bf16[16,64,2,1024]{3,2,1,0:T(2,128)(2,1)} %bitcast.37), slice={[0:16], [0:32], [0:2], [0:1024]} | slice | bytes 4194304 | tf_op jit(solution)/shard_map/slice | solution.py:428
  3.1 2.6 %reshape.100 = bf16[16,32,2,8,128]{4,3,2,1,0:T(8,128)(2,1)} reshape(bf16[16,32,2,1024]{3,2,1,0:T(2,128)(2,1)S(1)} %slice.32) | data formatting | bytes 4194304 | tf_op jit(solution)/shard_map/reshape | solution.py:428
  5.7 5.7 %all-to-all-start = ((bf16[16,32,2,8,128]{4,3,2,1,0:T(8,128)(2,1)}), bf16[16,32,2,8,128]{4,3,2,1,0:T(8,128)(2,1)S(1)}, u32[]{:S(2)}, u32[]{:S(2)}) async-start(bf16[16,32,2,8,128]{4,3,2,1,0:T(8,128)(2,1)} %reshape.100), calls=%async_computation | async-start | bytes 4194304 | tf_op jit(solution)/shard_map/all_to_all | solution.py:429
  12.3 4.5 %slice.33 = bf16[16,32,2,1024]{3,2,1,0:T(2,128)(2,1)} slice(bf16[16,64,2,1024]{3,2,1,0:T(2,128)(2,1)} %bitcast.38), slice={[0:16], [32:64], [0:2], [0:1024]} | slice | bytes 4194304 | tf_op jit(solution)/shard_map/slice | solution.py:428
  16.7 4.4 %reshape.103 = bf16[16,32,2,8,128]{4,3,2,1,0:T(8,128)(2,1)} reshape(bf16[16,32,2,1024]{3,2,1,0:T(2,128)(2,1)} %slice.33) | data formatting | bytes 4194304 | tf_op jit(solution)/shard_map/reshape | solution.py:428
  22.7 17.2 %all-to-all-done.refs_2_ = bf16[16,32,2,8,128]{4,3,2,1,0:T(8,128)(2,1)S(1)} async-done(((bf16[16,32,2,8,128]{4,3,2,1,0:T(8,128)(2,1)}), bf16[16,32,2,8,128]{4,3,2,1,0:T(8,128)(2,1)S(1)}, u32[]{:S(2)}, u32[]{:S(2)}) %all-to-all-start) | async-done | bytes 2097184 | tf_op jit(solution)/shard_map/all_to_all | solution.py:429
  40.0 4.3 %all-to-all-start.2 = ((bf16[16,32,2,8,128]{4,3,2,1,0:T(8,128)(2,1)}), bf16[16,32,2,8,128]{4,3,2,1,0:T(8,128)(2,1)}, u32[]{:S(2)}, u32[]{:S(2)}) async-start(bf16[16,32,2,8,128]{4,3,2,1,0:T(8,128)(2,1)} %reshape.103), calls=%async_computation.2 | async-start | bytes 4194304 | tf_op jit(solution)/shard_map/all_to_all | solution.py:429
  46.2 7.8 %reshape.101.refs_3_ = bf16[64,2,128,128]{3,2,1,0:T(8,128)(2,1)} reshape(bf16[64,2,16384]{2,1,0:T(2,128)(2,1)} %param.20) | data formatting | bytes 8388608 | tf_op jit(solution)/shard_map/reshape | solution.py:417
  54.0 21.2 %shard_map.181 = (bf16[16,2,128,128]{3,2,1,0:T(8,128)(2,1)}, bf16[16,1,128,128]{3,2,1,0:T(8,128)(2,1)}, bf16[16,3,128,128]{3,2,1,0:T(8,128)(2,1)}) custom-call(s32[512]{0:T(512)} %reshape.97.refs_0_, s32[512]{0:T(512)} %reshape.98.refs_1_, bf16[16,32,2,8,128]{4,3,2,1,0:T(8,128)(2,1)} %copy-done.4, bf16[64,2,128,128]{3,2,1,0:T(8,128)(2,1)} %reshape.101.refs_3_, ...), custom_call_target="tpu_custom_call" | custom-call | tf_op jit(solution)/shard_map/pallas_call | solution.py:146
  76.6 2.4 %collective-permute-start.1 = (bf16[16,1,128,128]{3,2,1,0:T(8,128)(2,1)}, bf16[16,1,128,128]{3,2,1,0:T(8,128)(2,1)S(1)}, u32[]{:S(2)}, u32[]{:S(2)}) collective-permute-start(bf16[16,1,128,128]{3,2,1,0:T(8,128)(2,1)} %get-tuple-element.14), channel_id=1, source_target_pairs={{16,0},{17,1},{18,2},{19,3},{20,4},{21,5},{22,6},{32,16},{33,17},{... | collective-permute-start | bytes 1572872 | tf_op jit(solution)/shard_map/ppermute | solution.py:436
  79.2 14.5 %collective-permute-done.1.far_ref = bf16[16,1,128,128]{3,2,1,0:T(8,128)(2,1)S(1)} collective-permute-done((bf16[16,1,128,128]{3,2,1,0:T(8,128)(2,1)}, bf16[16,1,128,128]{3,2,1,0:T(8,128)(2,1)S(1)}, u32[]{:S(2)}, u32[]{:S(2)}) %collective-permute-start.1) | collective-permute-done | bytes 524320 | tf_op jit(solution)/shard_map/ppermute | solution.py:436
  93.7 4.4 %collective-permute-done.near_ref = bf16[16,2,128,128]{3,2,1,0:T(8,128)(2,1)S(1)} collective-permute-done((bf16[16,2,128,128]{3,2,1,0:T(8,128)(2,1)}, bf16[16,2,128,128]{3,2,1,0:T(8,128)(2,1)S(1)}, u32[]{:S(2)}, u32[]{:S(2)}) %collective-permute-start) | collective-permute-done | bytes 1048608 | tf_op jit(solution)/shard_map/ppermute | solution.py:436
  98.1 1.4 copy-done.2
  99.5 2.2 %shard_map.182 = bf16[16,3,128,128]{3,2,1,0:T(8,128)(2,1)} custom-call(s32[128]{0:T(128)S(1)} %reshape.96.flag_ref, bf16[16,3,128,128]{3,2,1,0:T(8,128)(2,1)S(1)} %copy-done.2, bf16[16,2,128,128]{3,2,1,0:T(8,128)(2,1)S(1)} %collective-permute-done.near_ref, bf16[16,1,128,128]{3,2,1,0:T(8,128)(2,1)S(1)} %collective-permute-done.1.far_ref), custom_call_target="tpu_custom_call" | custom-call | tf_op jit(solution)/shard_map/pallas_call | solution.py:283
  101.7 10.3 %all-to-all-start.1 = ((bf16[16,3,128,128]{3,2,1,0:T(8,128)(2,1)}), bf16[16,3,128,128]{3,2,1,0:T(8,128)(2,1)S(1)}, u32[]{:S(2)}, u32[]{:S(2)}) async-start(bf16[16,3,128,128]{3,2,1,0:T(8,128)(2,1)} %shard_map.182), calls=%async_computation.1 | async-start | bytes 3145728 | tf_op jit(solution)/shard_map/all_to_all | solution.py:440
  112.0 21.3 %shard_map.183 = (bf16[16,2,128,128]{3,2,1,0:T(8,128)(2,1)}, bf16[16,1,128,128]{3,2,1,0:T(8,128)(2,1)}, bf16[16,3,128,128]{3,2,1,0:T(8,128)(2,1)}) custom-call(s32[512]{0:T(512)} %reshape.97.refs_0_, s32[512]{0:T(512)} %reshape.98.refs_1_, bf16[16,32,2,8,128]{4,3,2,1,0:T(8,128)(2,1)} %all-to-all-done.2.refs_2_, bf16[64,2,128,128]{3,2,1,0:T(8,128)(2,1)} %reshape.101.refs_3_, ...), custom_call_target="tpu_custom_call" | custom-call | tf_op jit(solution)/shard_map/pallas_call | solution.py:146
  134.6 1.9 collective-permute-start.3
  136.6 15.7 %collective-permute-done.3.far_ref = bf16[16,1,128,128]{3,2,1,0:T(8,128)(2,1)S(1)} collective-permute-done((bf16[16,1,128,128]{3,2,1,0:T(8,128)(2,1)}, bf16[16,1,128,128]{3,2,1,0:T(8,128)(2,1)S(1)}, u32[]{:S(2)}, u32[]{:S(2)}) %collective-permute-start.3) | collective-permute-done | bytes 524320 | tf_op jit(solution)/shard_map/ppermute | solution.py:436
  152.2 4.2 %collective-permute-done.2.near_ref = bf16[16,2,128,128]{3,2,1,0:T(8,128)(2,1)S(1)} collective-permute-done((bf16[16,2,128,128]{3,2,1,0:T(8,128)(2,1)}, bf16[16,2,128,128]{3,2,1,0:T(8,128)(2,1)S(1)}, u32[]{:S(2)}, u32[]{:S(2)}) %collective-permute-start.2) | collective-permute-done | bytes 1048608 | tf_op jit(solution)/shard_map/ppermute | solution.py:436
  156.4 1.4 copy-done.3
  157.8 2.2 %shard_map.184 = bf16[16,3,128,128]{3,2,1,0:T(8,128)(2,1)} custom-call(s32[128]{0:T(128)S(1)} %reshape.96.flag_ref, bf16[16,3,128,128]{3,2,1,0:T(8,128)(2,1)S(1)} %copy-done.3, bf16[16,2,128,128]{3,2,1,0:T(8,128)(2,1)S(1)} %collective-permute-done.2.near_ref, bf16[16,1,128,128]{3,2,1,0:T(8,128)(2,1)S(1)} %collective-permute-done.3.far_ref), custom_call_target="tpu_custom_call" | custom-call | tf_op jit(solution)/shard_map/pallas_call | solution.py:283
  160.0 10.6 %all-to-all-start.3 = ((bf16[16,3,128,128]{3,2,1,0:T(8,128)(2,1)}), bf16[16,3,128,128]{3,2,1,0:T(8,128)(2,1)}, u32[]{:S(2)}, u32[]{:S(2)}) async-start(bf16[16,3,128,128]{3,2,1,0:T(8,128)(2,1)} %shard_map.184), calls=%async_computation.3 | async-start | bytes 3145728 | tf_op jit(solution)/shard_map/all_to_all | solution.py:440
  170.9 21.1 %all-to-all-done.3.second_ref = bf16[16,3,128,128]{3,2,1,0:T(8,128)(2,1)} async-done(((bf16[16,3,128,128]{3,2,1,0:T(8,128)(2,1)}), bf16[16,3,128,128]{3,2,1,0:T(8,128)(2,1)}, u32[]{:S(2)}, u32[]{:S(2)}) %all-to-all-start.3) | async-done | bytes 1572896 | tf_op jit(solution)/shard_map/all_to_all | solution.py:440
  192.0 8.4 %cross.1 = f32[4,2,512,128]{3,2,1,0:T(8,128)} custom-call(s32[8]{0:T(128)S(1)} %reshape.95.info_ref, bf16[16,3,128,128]{3,2,1,0:T(8,128)(2,1)S(1)} %all-to-all-done.1.first_ref, bf16[16,3,128,128]{3,2,1,0:T(8,128)(2,1)} %all-to-all-done.3.second_ref, bf16[512,1024]{1,0:T(8,128)(2,1)S(1)} %copy-done, bf16[256,256]{1,0:T(8,128)(2,1)S(1)} %copy-done.1), custom_call_target="tpu_custom_call" | custom-call | tf_op jit(solution)/shard_map/cross/pallas_call | solution.py:339
  (47 shorter events, 7.3 us)
Async XLA Ops:
  5.7 6.5 %copy-start.5 = (s32[8,63]{1,0:T(8,128)S(1)}, s32[8,63]{1,0:T(8,128)}, u32[]{:S(2)}) copy-start(s32[8,63]{1,0:T(8,128)} %param.22) | copy-start | bytes 6052
  5.7 34.2 %all-to-all-start = ((bf16[16,32,2,8,128]{4,3,2,1,0:T(8,128)(2,1)}), bf16[16,32,2,8,128]{4,3,2,1,0:T(8,128)(2,1)S(1)}, u32[]{:S(2)}, u32[]{:S(2)}) async-start(bf16[16,32,2,8,128]{4,3,2,1,0:T(8,128)(2,1)} %reshape.100), calls=%async_computation | async-start | bytes 4194304 | tf_op jit(solution)/shard_map/all_to_all | solution.py:429
  40.0 4.4 %copy-start.4 = (bf16[16,32,2,8,128]{4,3,2,1,0:T(8,128)(2,1)}, bf16[16,32,2,8,128]{4,3,2,1,0:T(8,128)(2,1)S(1)}, u32[]{:S(2)}) copy-start(bf16[16,32,2,8,128]{4,3,2,1,0:T(8,128)(2,1)S(1)} %all-to-all-done.refs_2_) | copy-start | bytes 6291460
  40.0 61.7 %all-to-all-start.2 = ((bf16[16,32,2,8,128]{4,3,2,1,0:T(8,128)(2,1)}), bf16[16,32,2,8,128]{4,3,2,1,0:T(8,128)(2,1)}, u32[]{:S(2)}, u32[]{:S(2)}) async-start(bf16[16,32,2,8,128]{4,3,2,1,0:T(8,128)(2,1)} %reshape.103), calls=%async_computation.2 | async-start | bytes 4194304 | tf_op jit(solution)/shard_map/all_to_all | solution.py:429
  75.2 22.9 %collective-permute-start = (bf16[16,2,128,128]{3,2,1,0:T(8,128)(2,1)}, bf16[16,2,128,128]{3,2,1,0:T(8,128)(2,1)S(1)}, u32[]{:S(2)}, u32[]{:S(2)}) collective-permute-start(bf16[16,2,128,128]{3,2,1,0:T(8,128)(2,1)} %get-tuple-element.13), channel_id=1, source_target_pairs={{16,8},{17,9},{18,10},{19,11},{20,12},{21,13},{22,14},{32,24},{33,... | collective-permute-start | bytes 3145736 | tf_op jit(solution)/shard_map/ppermute | solution.py:436
  76.6 17.1 %collective-permute-start.1 = (bf16[16,1,128,128]{3,2,1,0:T(8,128)(2,1)}, bf16[16,1,128,128]{3,2,1,0:T(8,128)(2,1)S(1)}, u32[]{:S(2)}, u32[]{:S(2)}) collective-permute-start(bf16[16,1,128,128]{3,2,1,0:T(8,128)(2,1)} %get-tuple-element.14), channel_id=1, source_target_pairs={{16,0},{17,1},{18,2},{19,3},{20,4},{21,5},{22,6},{32,16},{33,17},{... | collective-permute-start | bytes 1572872 | tf_op jit(solution)/shard_map/ppermute | solution.py:436
  98.1 1.4 copy-start.2
  101.7 58.3 %all-to-all-start.1 = ((bf16[16,3,128,128]{3,2,1,0:T(8,128)(2,1)}), bf16[16,3,128,128]{3,2,1,0:T(8,128)(2,1)S(1)}, u32[]{:S(2)}, u32[]{:S(2)}) async-start(bf16[16,3,128,128]{3,2,1,0:T(8,128)(2,1)} %shard_map.182), calls=%async_computation.1 | async-start | bytes 3145728 | tf_op jit(solution)/shard_map/all_to_all | solution.py:440
  133.3 23.1 %collective-permute-start.2 = (bf16[16,2,128,128]{3,2,1,0:T(8,128)(2,1)}, bf16[16,2,128,128]{3,2,1,0:T(8,128)(2,1)S(1)}, u32[]{:S(2)}, u32[]{:S(2)}) collective-permute-start(bf16[16,2,128,128]{3,2,1,0:T(8,128)(2,1)} %get-tuple-element.17), channel_id=1, source_target_pairs={{16,8},{17,9},{18,10},{19,11},{20,12},{21,13},{22,14},{32,24},{33,... | collective-permute-start | bytes 3145736 | tf_op jit(solution)/shard_map/ppermute | solution.py:436
  134.6 17.6 %collective-permute-start.3 = (bf16[16,1,128,128]{3,2,1,0:T(8,128)(2,1)}, bf16[16,1,128,128]{3,2,1,0:T(8,128)(2,1)S(1)}, u32[]{:S(2)}, u32[]{:S(2)}) collective-permute-start(bf16[16,1,128,128]{3,2,1,0:T(8,128)(2,1)} %get-tuple-element.18), channel_id=1, source_target_pairs={{16,0},{17,1},{18,2},{19,3},{20,4},{21,5},{22,6},{32,16},{33,17},{... | collective-permute-start | bytes 1572872 | tf_op jit(solution)/shard_map/ppermute | solution.py:436
  156.4 1.4 copy-start.3
  160.0 32.0 %copy-start = (bf16[512,1024]{1,0:T(8,128)(2,1)S(1)}, bf16[512,1024]{1,0:T(8,128)(2,1)}, u32[]{:S(2)}) copy-start(bf16[512,1024]{1,0:T(8,128)(2,1)} %constant.62.clone.refs_9_.w_ref) | copy-start | bytes 3145732
  160.0 32.0 %copy-start.1 = (bf16[256,256]{1,0:T(8,128)(2,1)S(1)}, bf16[256,256]{1,0:T(8,128)(2,1)}, u32[]{:S(2)}) copy-start(bf16[256,256]{1,0:T(8,128)(2,1)} %constant.59.clone.refs_4_.refs_6_.l_ref) | copy-start | bytes 393220
  160.0 32.0 %all-to-all-start.3 = ((bf16[16,3,128,128]{3,2,1,0:T(8,128)(2,1)}), bf16[16,3,128,128]{3,2,1,0:T(8,128)(2,1)}, u32[]{:S(2)}, u32[]{:S(2)}) async-start(bf16[16,3,128,128]{3,2,1,0:T(8,128)(2,1)} %shard_map.184), calls=%async_computation.3 | async-start | bytes 3145728 | tf_op jit(solution)/shard_map/all_to_all | solution.py:440
where the time goes:
time: 202 us; the launch traced here: 200 us
  waiting for transfers between devices  77 us (38%)
  Pallas kernels  55.3 us (27%)
  starting transfers between devices  38 us (19%)
  local copies, waits for them, and re-layouts  28.8 us (14%)
    pallas_call x2, Pallas kernels, focus(): pl.pallas_call(lambda *refs: focus_kernel(*refs, steps=steps, turns=turns...  42.5 us
    ppermute x4, waiting for transfers between devices, staged(): passed.append(lax.ppermute(parts[way], ('rng', 'az'), reach[way]))  38.7 us
    all_to_all x2, waiting for transfers between devices, staged(): lax.all_to_all(joined, 'az', split_axis=0, concat_axis=0, tiled=True)  21.1 us
    all_to_all x2, starting transfers between devices, staged(): lax.all_to_all(joined, 'az', split_axis=0, concat_axis=0, tiled=True)  20.9 us
    all_to_all x2, waiting for transfers between devices, staged(): lax.all_to_all(chosen, 'az', split_axis=0, concat_axis=0, tiled=True)  17.2 us
    all_to_all x2, starting transfers between devices, staged(): lax.all_to_all(chosen, 'az', split_axis=0, concat_axis=0, tiled=True)  10 us
    pallas_call x1, Pallas kernels, cross(): pl.pallas_call(cross_kernel, out_shape=jax.ShapeDtypeStruct((IMG_DEV, 2,...  8.43 us
    reshape x1, local copies, waits for them, and re-layouts, staged(): response = azimuth_filter.reshape(COL, 2, AZ_OUTER, AZ_INNER)  7.82 us
  transfers between devices with their start and end apart: 8, of which 6 were waited for; matrix products, arithmetic and copies ran while one was open for 11% of the time, Pallas kernels for 23%

commit v1 on v0

--- a/solution.py
+++ b/solution.py
@@ -21,7 +21,7 @@
 BLOCK = 16
 TURN_ROWS = 32
 HALF = COL // 2
-DEEP = 2
+DEEP = 4
 NEAR = 2
 epsilon = 1e-06
 bf16 = jnp.bfloat16
@@ -64,9 +64,9 @@
     return jnp.dot(left, right, preferred_element_type=f32)
 
 
-def focus_kernel(beyond_ref, own_ref, *refs, steps, turns):
+def focus_kernel(info_ref, *refs, steps, turns):
     arr_ref, filt_ref, l1_ref, t2_ref, t3_ref, l4_ref, tw_ref, w_ref, near_ref, far_ref, kept_ref = refs[:11]
-    y_ref, lines_ref, list_ref, *spec_refs = refs[11:]
+    y_ref, lines_ref, stage_ref, list_ref, *spec_refs = refs[11:]
     step = pl.program_id(0)
 
     @pl.when(step < steps)
@@ -133,12 +133,18 @@
 
     @pl.when(step == steps + turns - 1)
     def _():
-        for info_ref, outs in ((beyond_ref, (near_ref, far_ref)), (own_ref, (kept_ref,))):
-            trips = listed_trips(info_ref, list_ref)
-            look_trips(trips, info_ref, list_ref, lines_ref, spec_refs, w_ref, l4_ref, outs)
-
-
-def focus(beyond, own, arrived, response, half):
+        look_trips(info_ref, list_ref, lines_ref, stage_ref, spec_refs, w_ref, l4_ref)
+
+        def handed(owner, carry):
+            near_ref[owner] = stage_ref[owner, :NEAR]
+            far_ref[owner] = stage_ref[owner, NEAR:]
+            kept_ref[owner] = stage_ref[16 + owner]
+            return carry
+
+        lax.fori_loop(0, 16, handed, 0)
+
+
+def focus(info, arrived, response, half):
     steps = HALF // BLOCK
     turns = AZ_OUTER // TURN_ROWS
     whole = lambda shape: pl.BlockSpec(shape, lambda i, *s: (0,) * len(shape))
@@ -147,7 +153,7 @@
         lambda *refs: focus_kernel(*refs, steps=steps, turns=turns),
         out_shape=[jax.ShapeDtypeStruct(shape, bf16) for shape in shapes],
         grid_spec=pltpu.PrefetchScalarGridSpec(
-            num_scalar_prefetch=2,
+            num_scalar_prefetch=1,
             grid=(steps + turns,),
             in_specs=[
                 pl.BlockSpec((16, BLOCK, 2, 8, 128), lambda i, *s: (0, jnp.minimum(i, steps - 1), 0, 0, 0)),
@@ -165,13 +171,13 @@
             scratch_shapes=[
                 pltpu.VMEM((2 * HALF * 128, 128), f32),
                 pltpu.VMEM((LINES, 128), f32),
-                pltpu.SMEM((IMG_DEV * (16 + 2 * DEEP),), jnp.int32),
+                pltpu.VMEM((32, 3, LOOK, 128), bf16),
+                pltpu.SMEM((2 * 16 * IMG_DEV + 8,), jnp.int32),
             ]
             + [pltpu.VMEM((2 * IMG_L, 128), f32)] * DEEP,
         ),
     )(
-        beyond,
-        own,
+        info,
         arrived,
         response,
         jnp.asarray(left_form(128, -1.0)),
@@ -183,39 +189,27 @@
     )
 
 
-def listed_trips(info_ref, list_ref):
-    owners = 16
-    room = owners + 2 * DEEP
-    most = 0
-    for slot in range(IMG_DEV):
-        for place in range(room):
-            list_ref[slot * room + place] = 0
-        found = 0
-        for owner in range(owners):
-            list_ref[slot * room + found] = owner
-            found = found + info_ref[(owner * IMG_DEV + slot) * 8 + 1]
-        most = jnp.maximum(most, found)
-    return (most + DEEP - 1) // DEEP
-
-
-def look_trips(trips, info_ref, list_ref, lines_ref, spec_refs, w_ref, u_ref, outs):
-    room = 16 + 2 * DEEP
+def look_trips(info_ref, list_ref, lines_ref, stage_ref, spec_refs, w_ref, u_ref):
     lane = lax.broadcasted_iota(jnp.int32, (1, 128), 1)
     low_lanes = lane < 64
     sign = jnp.where(low_lanes, 1.0, -1.0).astype(f32)
     even = lane % 64 < 32
-    split = len(outs) > 1
+    quarter = lane // HALF
+    found = 0
+    for entry in range(2 * 16 * IMG_DEV):
+        list_ref[found] = entry
+        found = found + info_ref[entry * 8 + 1]
 
     def chosen(tiles):
         return jnp.where(low_lanes, jnp.where(even, tiles[0], tiles[1]), jnp.where(even, tiles[2], tiles[3]))
 
-    def trip(at, carry):
+    def trip(first, deep):
         picks = [
-            [list_ref[slot * room + DEEP * at + nth] for slot in range(IMG_DEV)] for nth in range(DEEP)
+            [list_ref[jnp.minimum(first + nth * 4 + spot, found - 1)] for spot in range(4)]
+            for nth in range(deep)
         ]
-        places = [[(owner * IMG_DEV + slot) * 8 for slot, owner in enumerate(row)] for row in picks]
-        for nth in range(DEEP):
-            images = [lines_ref[pl.ds(info_ref[place], IMG_L), :] for place in places[nth]]
+        for nth in range(deep):
+            images = [lines_ref[pl.ds(info_ref[entry * 8], IMG_L), :] for entry in picks[nth]]
             near = jnp.where(even, images[0], images[1])
             far = jnp.where(even, images[2], images[3])
             side = pltpu.roll(jnp.where(low_lanes, far, near), 64, 1) * sign
@@ -230,14 +224,14 @@
             spectra = dot(w_ref[...], right)
             spec_refs[nth][:IMG_L, :] = spectra[:, :128]
             spec_refs[nth][IMG_L:, :] = spectra[:, 128:]
-        for nth in range(DEEP):
+        for nth in range(deep):
             columns = []
             for look in range(3):
                 parts = []
                 for part in (0, 1):
                     tiles = [
-                        spec_refs[nth][pl.ds(part * IMG_L + info_ref[place + 2 + look], LOOK), :]
-                        for place in places[nth]
+                        spec_refs[nth][pl.ds(part * IMG_L + info_ref[entry * 8 + 2 + look], LOOK), :]
+                        for entry in picks[nth]
                     ]
                     parts.append(chosen(tiles).astype(bf16))
                 columns.append(jnp.concatenate(parts, axis=0))
@@ -245,16 +239,24 @@
             for look in range(3):
                 re = value[:LOOK, look * 128 : look * 128 + 128]
                 im = value[LOOK:, look * 128 : look * 128 + 128]
-                power = (re * re + im * im).astype(bf16)
-                for slot, owner in enumerate(picks[nth]):
-                    lanes = slice(slot * HALF, slot * HALF + HALF)
-                    if split and look >= NEAR:
-                        outs[1][owner, look - NEAR, :, lanes] = power[:, lanes]
-                    else:
-                        outs[0][owner, look, :, lanes] = power[:, lanes]
+                power = re * re + im * im
+                for spot, entry in enumerate(picks[nth]):
+                    slot = entry % IMG_DEV
+                    placed = pltpu.roll(power, (HALF * (slot - spot + IMG_DEV)) % 128, 1).astype(bf16)
+                    row = entry // IMG_DEV
+                    stage_ref[row, look] = jnp.where(quarter == slot, placed, stage_ref[row, look])
+
+    def wide(at, carry):
+        trip(at * 4 * DEEP, DEEP)
         return carry
 
-    lax.fori_loop(0, trips, trip, 0)
+    def narrow(at, carry):
+        trip(most * 4 * DEEP, DEEP // 2)
+        return carry
+
+    most = (found + 2 * DEEP - 1) // (4 * DEEP)
+    lax.fori_loop(0, most, wide, 0)
+    lax.fori_loop(0, (found > most * 4 * DEEP).astype(jnp.int32), narrow, 0)
 
 
 def window_table():
@@ -412,7 +414,7 @@
         anchors, owners, look_bands, jnp.maximum(strip - 1, 0), count
     )
     keep = reaches(start, filled, column + count) * (strip > 0).astype(jnp.int32)
-    beyond = listed(line, bands, keep)
+    info = jnp.concatenate([listed(line, bands, keep), own])
 
     response = azimuth_filter.reshape(COL, 2, AZ_OUTER, AZ_INNER)
     reach = [
@@ -430,7 +432,7 @@
     kept = []
     passed = []
     for half in (0, 1):
-        *parts, mine_part = focus(beyond, own, arrived[half], response, half)
+        *parts, mine_part = focus(info, arrived[half], response, half)
         kept.append(mine_part)
         for way in (0, 1):
             passed.append(lax.ppermute(parts[way], ("rng", "az"), reach[way]))

time: 202 us -> 197 us (0.975)
  Pallas kernels: 55.3 us -> 48.7 us
  waiting for transfers between devices: 77 us -> 79.4 us
    pallas_call x2, Pallas kernels: 42.5 us -> 35.9 us  [focus(): pl.pallas_call(lambda *refs: focus_kernel(*refs, steps=steps, turns=turns...]
    ppermute x4, waiting for transfers between devices: 38.7 us -> 41.3 us  [staged(): passed.append(lax.ppermute(parts[way], ('rng', 'az'), reach[way]))]
  transfers between devices with their start and end apart: 8 -> 8, of which waited for: 6 -> 6; matrix products, arithmetic and copies ran while one was open for 11% -> 10% of each run, Pallas kernels for 23% -> 21%
where the time goes in v1:
time: 197 us; the launch traced here: 196 us
  waiting for transfers between devices  79.4 us (40%)
  Pallas kernels  48.7 us (25%)
  starting transfers between devices  38.3 us (19%)
  local copies, waits for them, and re-layouts  28.2 us (14%)
    ppermute x4, waiting for transfers between devices, staged(): passed.append(lax.ppermute(parts[way], ('rng', 'az'), reach[way]))  41.3 us
    pallas_call x2, Pallas kernels, focus(): pl.pallas_call(lambda *refs: focus_kernel(*refs, steps=steps, turns=turns...  35.9 us
    all_to_all x2, waiting for transfers between devices, staged(): lax.all_to_all(joined, 'az', split_axis=0, concat_axis=0, tiled=True)  21.1 us
    all_to_all x2, starting transfers between devices, staged(): lax.all_to_all(joined, 'az', split_axis=0, concat_axis=0, tiled=True)  21 us
    all_to_all x2, waiting for transfers between devices, staged(): lax.all_to_all(chosen, 'az', split_axis=0, concat_axis=0, tiled=True)  17 us
    all_to_all x2, starting transfers between devices, staged(): lax.all_to_all(chosen, 'az', split_axis=0, concat_axis=0, tiled=True)  10 us
    pallas_call x1, Pallas kernels, cross(): pl.pallas_call(cross_kernel, out_shape=jax.ShapeDtypeStruct((IMG_DEV, 2,...  8.43 us
    reshape x1, local copies, waits for them, and re-layouts, staged(): response = azimuth_filter.reshape(COL, 2, AZ_OUTER, AZ_INNER)  7.84 us
  transfers between devices with their start and end apart: 8, of which 6 were waited for; matrix products, arithmetic and copies ran while one was open for 10% of the time, Pallas kernels for 21%

profile of v1, /device:TPU:50, one launch (start us, length us, event | category | flops | bytes accessed | tf_op | source)
XLA Modules:
  0.0 195.9 jit_solution(13362388708675306283)
XLA Ops:
  0.0 3.1 %slice.32 = bf16[16,32,2,1024]{3,2,1,0:T(2,128)(2,1)S(1)} slice(bf16[16,64,2,1024]{3,2,1,0:T(2,128)(2,1)} %bitcast.37), slice={[0:16], [0:32], [0:2], [0:1024]} | slice | bytes 4194304 | tf_op jit(solution)/shard_map/slice | solution.py:430
  3.1 2.6 %reshape.100 = bf16[16,32,2,8,128]{4,3,2,1,0:T(8,128)(2,1)} reshape(bf16[16,32,2,1024]{3,2,1,0:T(2,128)(2,1)S(1)} %slice.32) | data formatting | bytes 4194304 | tf_op jit(solution)/shard_map/reshape | solution.py:430
  5.7 5.7 %all-to-all-start = ((bf16[16,32,2,8,128]{4,3,2,1,0:T(8,128)(2,1)}), bf16[16,32,2,8,128]{4,3,2,1,0:T(8,128)(2,1)S(1)}, u32[]{:S(2)}, u32[]{:S(2)}) async-start(bf16[16,32,2,8,128]{4,3,2,1,0:T(8,128)(2,1)} %reshape.100), calls=%async_computation | async-start | bytes 4194304 | tf_op jit(solution)/shard_map/all_to_all | solution.py:431
  13.0 4.5 %slice.33 = bf16[16,32,2,1024]{3,2,1,0:T(2,128)(2,1)} slice(bf16[16,64,2,1024]{3,2,1,0:T(2,128)(2,1)} %bitcast.38), slice={[0:16], [32:64], [0:2], [0:1024]} | slice | bytes 4194304 | tf_op jit(solution)/shard_map/slice | solution.py:430
  17.5 4.4 %reshape.103 = bf16[16,32,2,8,128]{4,3,2,1,0:T(8,128)(2,1)} reshape(bf16[16,32,2,1024]{3,2,1,0:T(2,128)(2,1)} %slice.33) | data formatting | bytes 4194304 | tf_op jit(solution)/shard_map/reshape | solution.py:430
  22.9 17.0 %all-to-all-done.refs_1_ = bf16[16,32,2,8,128]{4,3,2,1,0:T(8,128)(2,1)S(1)} async-done(((bf16[16,32,2,8,128]{4,3,2,1,0:T(8,128)(2,1)}), bf16[16,32,2,8,128]{4,3,2,1,0:T(8,128)(2,1)S(1)}, u32[]{:S(2)}, u32[]{:S(2)}) %all-to-all-start) | async-done | bytes 2097184 | tf_op jit(solution)/shard_map/all_to_all | solution.py:431
  40.0 4.3 %all-to-all-start.2 = ((bf16[16,32,2,8,128]{4,3,2,1,0:T(8,128)(2,1)}), bf16[16,32,2,8,128]{4,3,2,1,0:T(8,128)(2,1)}, u32[]{:S(2)}, u32[]{:S(2)}) async-start(bf16[16,32,2,8,128]{4,3,2,1,0:T(8,128)(2,1)} %reshape.103), calls=%async_computation.2 | async-start | bytes 4194304 | tf_op jit(solution)/shard_map/all_to_all | solution.py:431
  44.8 7.8 %reshape.101.refs_2_ = bf16[64,2,128,128]{3,2,1,0:T(8,128)(2,1)} reshape(bf16[64,2,16384]{2,1,0:T(2,128)(2,1)} %param.20) | data formatting | bytes 8388608 | tf_op jit(solution)/shard_map/reshape | solution.py:419
  53.2 18.0 %shard_map.181 = (bf16[16,2,128,128]{3,2,1,0:T(8,128)(2,1)}, bf16[16,1,128,128]{3,2,1,0:T(8,128)(2,1)}, bf16[16,3,128,128]{3,2,1,0:T(8,128)(2,1)}) custom-call(s32[1024]{0:T(1024)} %copy-done.5, bf16[16,32,2,8,128]{4,3,2,1,0:T(8,128)(2,1)} %copy-done.4, bf16[64,2,128,128]{3,2,1,0:T(8,128)(2,1)} %reshape.101.refs_2_, ...), custom_call_target="tpu_custom_call" | custom-call | tf_op jit(solution)/shard_map/pallas_call | solution.py:152
  72.5 2.6 %collective-permute-start.1 = (bf16[16,1,128,128]{3,2,1,0:T(8,128)(2,1)}, bf16[16,1,128,128]{3,2,1,0:T(8,128)(2,1)S(1)}, u32[]{:S(2)}, u32[]{:S(2)}) collective-permute-start(bf16[16,1,128,128]{3,2,1,0:T(8,128)(2,1)} %get-tuple-element.14), channel_id=1, source_target_pairs={{16,0},{17,1},{18,2},{19,3},{20,4},{21,5},{22,6},{32,16},{33,17},{... | collective-permute-start | bytes 1572872 | tf_op jit(solution)/shard_map/ppermute | solution.py:438
  75.4 15.7 %collective-permute-done.1.far_ref = bf16[16,1,128,128]{3,2,1,0:T(8,128)(2,1)S(1)} collective-permute-done((bf16[16,1,128,128]{3,2,1,0:T(8,128)(2,1)}, bf16[16,1,128,128]{3,2,1,0:T(8,128)(2,1)S(1)}, u32[]{:S(2)}, u32[]{:S(2)}) %collective-permute-start.1) | collective-permute-done | bytes 524320 | tf_op jit(solution)/shard_map/ppermute | solution.py:438
  91.1 4.4 %collective-permute-done.near_ref = bf16[16,2,128,128]{3,2,1,0:T(8,128)(2,1)S(1)} collective-permute-done((bf16[16,2,128,128]{3,2,1,0:T(8,128)(2,1)}, bf16[16,2,128,128]{3,2,1,0:T(8,128)(2,1)S(1)}, u32[]{:S(2)}, u32[]{:S(2)}) %collective-permute-start) | collective-permute-done | bytes 1048608 | tf_op jit(solution)/shard_map/ppermute | solution.py:438
  95.5 1.4 copy-done.2
  96.9 2.2 %shard_map.182 = bf16[16,3,128,128]{3,2,1,0:T(8,128)(2,1)} custom-call(s32[128]{0:T(128)S(1)} %reshape.96.flag_ref, bf16[16,3,128,128]{3,2,1,0:T(8,128)(2,1)S(1)} %copy-done.2, bf16[16,2,128,128]{3,2,1,0:T(8,128)(2,1)S(1)} %collective-permute-done.near_ref, bf16[16,1,128,128]{3,2,1,0:T(8,128)(2,1)S(1)} %collective-permute-done.1.far_ref), custom_call_target="tpu_custom_call" | custom-call | tf_op jit(solution)/shard_map/pallas_call | solution.py:285
  99.0 10.3 %all-to-all-start.1 = ((bf16[16,3,128,128]{3,2,1,0:T(8,128)(2,1)}), bf16[16,3,128,128]{3,2,1,0:T(8,128)(2,1)S(1)}, u32[]{:S(2)}, u32[]{:S(2)}) async-start(bf16[16,3,128,128]{3,2,1,0:T(8,128)(2,1)} %shard_map.182), calls=%async_computation.1 | async-start | bytes 3145728 | tf_op jit(solution)/shard_map/all_to_all | solution.py:442
  109.4 18.0 %shard_map.183 = (bf16[16,2,128,128]{3,2,1,0:T(8,128)(2,1)}, bf16[16,1,128,128]{3,2,1,0:T(8,128)(2,1)}, bf16[16,3,128,128]{3,2,1,0:T(8,128)(2,1)}) custom-call(s32[1024]{0:T(1024)} %copy-done.5, bf16[16,32,2,8,128]{4,3,2,1,0:T(8,128)(2,1)} %all-to-all-done.2.refs_1_, bf16[64,2,128,128]{3,2,1,0:T(8,128)(2,1)} %reshape.101.refs_2_, ...), custom_call_target="tpu_custom_call" | custom-call | tf_op jit(solution)/shard_map/pallas_call | solution.py:152
  128.7 1.9 collective-permute-start.3
  130.6 17.1 %collective-permute-done.3.far_ref = bf16[16,1,128,128]{3,2,1,0:T(8,128)(2,1)S(1)} collective-permute-done((bf16[16,1,128,128]{3,2,1,0:T(8,128)(2,1)}, bf16[16,1,128,128]{3,2,1,0:T(8,128)(2,1)S(1)}, u32[]{:S(2)}, u32[]{:S(2)}) %collective-permute-start.3) | collective-permute-done | bytes 524320 | tf_op jit(solution)/shard_map/ppermute | solution.py:438
  147.8 4.1 %collective-permute-done.2.near_ref = bf16[16,2,128,128]{3,2,1,0:T(8,128)(2,1)S(1)} collective-permute-done((bf16[16,2,128,128]{3,2,1,0:T(8,128)(2,1)}, bf16[16,2,128,128]{3,2,1,0:T(8,128)(2,1)S(1)}, u32[]{:S(2)}, u32[]{:S(2)}) %collective-permute-start.2) | collective-permute-done | bytes 1048608 | tf_op jit(solution)/shard_map/ppermute | solution.py:438
  151.9 1.4 copy-done.3
  153.3 2.2 %shard_map.184 = bf16[16,3,128,128]{3,2,1,0:T(8,128)(2,1)} custom-call(s32[128]{0:T(128)S(1)} %reshape.96.flag_ref, bf16[16,3,128,128]{3,2,1,0:T(8,128)(2,1)S(1)} %copy-done.3, bf16[16,2,128,128]{3,2,1,0:T(8,128)(2,1)S(1)} %collective-permute-done.2.near_ref, bf16[16,1,128,128]{3,2,1,0:T(8,128)(2,1)S(1)} %collective-permute-done.3.far_ref), custom_call_target="tpu_custom_call" | custom-call | tf_op jit(solution)/shard_map/pallas_call | solution.py:285
  155.5 10.7 %all-to-all-start.3 = ((bf16[16,3,128,128]{3,2,1,0:T(8,128)(2,1)}), bf16[16,3,128,128]{3,2,1,0:T(8,128)(2,1)}, u32[]{:S(2)}, u32[]{:S(2)}) async-start(bf16[16,3,128,128]{3,2,1,0:T(8,128)(2,1)} %shard_map.184), calls=%async_computation.3 | async-start | bytes 3145728 | tf_op jit(solution)/shard_map/all_to_all | solution.py:442
  166.4 21.1 %all-to-all-done.3.second_ref = bf16[16,3,128,128]{3,2,1,0:T(8,128)(2,1)} async-done(((bf16[16,3,128,128]{3,2,1,0:T(8,128)(2,1)}), bf16[16,3,128,128]{3,2,1,0:T(8,128)(2,1)}, u32[]{:S(2)}, u32[]{:S(2)}) %all-to-all-start.3) | async-done | bytes 1572896 | tf_op jit(solution)/shard_map/all_to_all | solution.py:442
  187.5 8.4 %cross.1 = f32[4,2,512,128]{3,2,1,0:T(8,128)} custom-call(s32[8]{0:T(128)S(1)} %reshape.95.info_ref, bf16[16,3,128,128]{3,2,1,0:T(8,128)(2,1)S(1)} %all-to-all-done.1.first_ref, bf16[16,3,128,128]{3,2,1,0:T(8,128)(2,1)} %all-to-all-done.3.second_ref, bf16[512,1024]{1,0:T(8,128)(2,1)S(1)} %copy-done, bf16[256,256]{1,0:T(8,128)(2,1)S(1)} %copy-done.1), custom_call_target="tpu_custom_call" | custom-call | tf_op jit(solution)/shard_map/cross/pallas_call | solution.py:341
  (52 shorter events, 6.7 us)
Async XLA Ops:
  5.7 7.2 %copy-start.6 = (s32[8,63]{1,0:T(8,128)S(1)}, s32[8,63]{1,0:T(8,128)}, u32[]{:S(2)}) copy-start(s32[8,63]{1,0:T(8,128)} %param.22) | copy-start | bytes 6052
  5.7 34.2 %all-to-all-start = ((bf16[16,32,2,8,128]{4,3,2,1,0:T(8,128)(2,1)}), bf16[16,32,2,8,128]{4,3,2,1,0:T(8,128)(2,1)S(1)}, u32[]{:S(2)}, u32[]{:S(2)}) async-start(bf16[16,32,2,8,128]{4,3,2,1,0:T(8,128)(2,1)} %reshape.100), calls=%async_computation | async-start | bytes 4194304 | tf_op jit(solution)/shard_map/all_to_all | solution.py:431
  40.0 4.4 %copy-start.4 = (bf16[16,32,2,8,128]{4,3,2,1,0:T(8,128)(2,1)}, bf16[16,32,2,8,128]{4,3,2,1,0:T(8,128)(2,1)S(1)}, u32[]{:S(2)}) copy-start(bf16[16,32,2,8,128]{4,3,2,1,0:T(8,128)(2,1)S(1)} %all-to-all-done.refs_1_) | copy-start | bytes 6291460
  40.0 59.1 %all-to-all-start.2 = ((bf16[16,32,2,8,128]{4,3,2,1,0:T(8,128)(2,1)}), bf16[16,32,2,8,128]{4,3,2,1,0:T(8,128)(2,1)}, u32[]{:S(2)}, u32[]{:S(2)}) async-start(bf16[16,32,2,8,128]{4,3,2,1,0:T(8,128)(2,1)} %reshape.103), calls=%async_computation.2 | async-start | bytes 4194304 | tf_op jit(solution)/shard_map/all_to_all | solution.py:431
  52.6 0.6 copy-start.5
  71.2 24.3 %collective-permute-start = (bf16[16,2,128,128]{3,2,1,0:T(8,128)(2,1)}, bf16[16,2,128,128]{3,2,1,0:T(8,128)(2,1)S(1)}, u32[]{:S(2)}, u32[]{:S(2)}) collective-permute-start(bf16[16,2,128,128]{3,2,1,0:T(8,128)(2,1)} %get-tuple-element.13), channel_id=1, source_target_pairs={{16,8},{17,9},{18,10},{19,11},{20,12},{21,13},{22,14},{32,24},{33,... | collective-permute-start | bytes 3145736 | tf_op jit(solution)/shard_map/ppermute | solution.py:438
  72.5 18.6 %collective-permute-start.1 = (bf16[16,1,128,128]{3,2,1,0:T(8,128)(2,1)}, bf16[16,1,128,128]{3,2,1,0:T(8,128)(2,1)S(1)}, u32[]{:S(2)}, u32[]{:S(2)}) collective-permute-start(bf16[16,1,128,128]{3,2,1,0:T(8,128)(2,1)} %get-tuple-element.14), channel_id=1, source_target_pairs={{16,0},{17,1},{18,2},{19,3},{20,4},{21,5},{22,6},{32,16},{33,17},{... | collective-permute-start | bytes 1572872 | tf_op jit(solution)/shard_map/ppermute | solution.py:438
  95.5 1.4 copy-start.2
  99.0 56.4 %all-to-all-start.1 = ((bf16[16,3,128,128]{3,2,1,0:T(8,128)(2,1)}), bf16[16,3,128,128]{3,2,1,0:T(8,128)(2,1)S(1)}, u32[]{:S(2)}, u32[]{:S(2)}) async-start(bf16[16,3,128,128]{3,2,1,0:T(8,128)(2,1)} %shard_map.182), calls=%async_computation.1 | async-start | bytes 3145728 | tf_op jit(solution)/shard_map/all_to_all | solution.py:442
  127.3 24.6 %collective-permute-start.2 = (bf16[16,2,128,128]{3,2,1,0:T(8,128)(2,1)}, bf16[16,2,128,128]{3,2,1,0:T(8,128)(2,1)S(1)}, u32[]{:S(2)}, u32[]{:S(2)}) collective-permute-start(bf16[16,2,128,128]{3,2,1,0:T(8,128)(2,1)} %get-tuple-element.17), channel_id=1, source_target_pairs={{16,8},{17,9},{18,10},{19,11},{20,12},{21,13},{22,14},{32,24},{33,... | collective-permute-start | bytes 3145736 | tf_op jit(solution)/shard_map/ppermute | solution.py:438
  128.7 19.1 %collective-permute-start.3 = (bf16[16,1,128,128]{3,2,1,0:T(8,128)(2,1)}, bf16[16,1,128,128]{3,2,1,0:T(8,128)(2,1)S(1)}, u32[]{:S(2)}, u32[]{:S(2)}) collective-permute-start(bf16[16,1,128,128]{3,2,1,0:T(8,128)(2,1)} %get-tuple-element.18), channel_id=1, source_target_pairs={{16,0},{17,1},{18,2},{19,3},{20,4},{21,5},{22,6},{32,16},{33,17},{... | collective-permute-start | bytes 1572872 | tf_op jit(solution)/shard_map/ppermute | solution.py:438
  151.9 1.4 copy-start.3
  155.5 32.0 %copy-start = (bf16[512,1024]{1,0:T(8,128)(2,1)S(1)}, bf16[512,1024]{1,0:T(8,128)(2,1)}, u32[]{:S(2)}) copy-start(bf16[512,1024]{1,0:T(8,128)(2,1)} %constant.62.clone.refs_8_.w_ref) | copy-start | bytes 3145732
  155.5 32.0 %copy-start.1 = (bf16[256,256]{1,0:T(8,128)(2,1)S(1)}, bf16[256,256]{1,0:T(8,128)(2,1)}, u32[]{:S(2)}) copy-start(bf16[256,256]{1,0:T(8,128)(2,1)} %constant.59.clone.refs_3_.refs_5_.l_ref) | copy-start | bytes 393220
  155.5 32.0 %all-to-all-start.3 = ((bf16[16,3,128,128]{3,2,1,0:T(8,128)(2,1)}), bf16[16,3,128,128]{3,2,1,0:T(8,128)(2,1)}, u32[]{:S(2)}, u32[]{:S(2)}) async-start(bf16[16,3,128,128]{3,2,1,0:T(8,128)(2,1)} %shard_map.184), calls=%async_computation.3 | async-start | bytes 3145728 | tf_op jit(solution)/shard_map/all_to_all | solution.py:442
